TPU v7x, 32 devices: a whole 2x2x4 slice. The times are simulated.
32 devices in a mesh: feat: 8 (over z, core), node: 4 (over y, x).
Axes of the slice: x: 2, y: 2, z: 4, core: 2. Of those that a mesh axis runs over, the one named last changes fastest.
Arguments:
- node_features: bfloat16 [1024, 4, 1024], P('feat', 'node'), may hold values from -6 to 6
- weight: bfloat16 [1024, 256], P('feat'), may hold values from -0.1875 to 0.1875
- out_bias: float32 [256], replicated, may hold values from -3 to 3
- edge_tiles: bfloat16 [4, 8, 8, 128, 128], P('node', 'feat'), may hold values from 0.049804688 to 1
- tile_column: int32 [4, 8, 8], P('node', 'feat'), may hold values from 0 to 7, as said below
- tile_count: int32 [4, 8], P('node', 'feat'), may hold values from 1 to 8, as said below
- grad_hidden: bfloat16 [4, 1024, 256], P('node', 'feat'), may hold values from -6 to 6
Outputs:
- hidden: bfloat16 [4, 1024, 256], P('node', 'feat')
- grad_features: bfloat16 [1024, 4, 1024], P('feat', 'node')
- weight_grad: float32 [1024, 256], P('feat')
Inputs may be any that keep to these rules, and one draw needn't show every extreme that they name: `tile_column`: the 8 column blocks listed for one row block are distinct, live slots or not. `tile_count`: slots of a row block beyond its count are ignored. In every cluster some row block has exactly 8 live tiles.
All inputs are finite; a program needn't handle non-finite values.
Results may differ from a plain program's by a relative error of at most 0.007.
Values may be sent and summed in bfloat16 or wider, within the bound.
A program may use at most 64 MiB of HBM per device.

v0:
```python
import math
import jax
import jax.numpy as jnp
from jax import lax
from jax.sharding import PartitionSpec as P


def gelu_tanh(pre_value):
    return jax.nn.gelu(pre_value, approximate=True)


def body(node_features, weight, out_bias, edge_tiles, tile_column, tile_count, grad_hidden):
    feat_dev, clusters, cluster_rows = node_features.shape
    blocks = lax.axis_size("feat")
    tile_rows = cluster_rows // blocks
    hidden_width = weight.shape[1]
    summed_rows = lax.psum_scatter(
        jnp.einsum("fqr,fh->rqh", node_features, weight, preferred_element_type=jnp.float32),
        "feat",
        scatter_dimension=0,
        tiled=True,
    )
    own_proj = jnp.transpose(summed_rows, (1, 0, 2))
    own_rounded = own_proj.astype(jnp.bfloat16)
    all_proj = lax.all_gather(own_rounded, "feat", axis=1, tiled=True)
    blocks_proj = all_proj.reshape(clusters, blocks, tile_rows, hidden_width)
    my_tiles = edge_tiles[:, 0]
    my_cols = tile_column[:, 0]
    counts = tile_count[:, 0]
    slot_ids = jnp.arange(my_tiles.shape[1], dtype=jnp.int32)
    live_mask = (slot_ids[None, :] < counts[:, None]).astype(jnp.bfloat16)
    masked = my_tiles * live_mask[:, :, None, None]
    degree = jnp.sum(masked, axis=(1, 3), dtype=jnp.float32)
    cluster_ids = jnp.arange(clusters, dtype=jnp.int32)[:, None]
    chosen = blocks_proj[cluster_ids, my_cols]
    summed = jnp.einsum("qsij,qsjh->qih", masked, chosen, preferred_element_type=jnp.float32)
    row_scale = lax.rsqrt(degree)[:, :, None]
    pre_act = summed * row_scale + out_bias
    activated, backward = jax.vjp(gelu_tanh, pre_act)
    hidden = activated.astype(jnp.bfloat16)
    (grad_pre,) = backward(grad_hidden.astype(jnp.float32))
    scaled = (grad_pre * row_scale).astype(jnp.bfloat16)
    tile_terms = jnp.einsum(
        "qsij,qih->qsjh", masked, scaled, preferred_element_type=jnp.float32
    ).astype(jnp.bfloat16)
    outgoing = (
        jnp.zeros((blocks, clusters, tile_rows, hidden_width), jnp.bfloat16)
        .at[my_cols, cluster_ids]
        .set(tile_terms)
    )
    arrived = lax.all_to_all(outgoing, "feat", split_axis=0, concat_axis=0, tiled=True)
    own_grad = jnp.sum(arrived, axis=0, dtype=jnp.float32).astype(jnp.bfloat16)
    all_grad = lax.all_gather(own_grad, "feat", axis=1, tiled=True)
    grad_features = jnp.einsum(
        "fh,qrh->fqr", weight, all_grad, preferred_element_type=jnp.float32
    ).astype(jnp.bfloat16)
    partial_grad = jnp.einsum(
        "fqr,qrh->fh", node_features, all_grad, preferred_element_type=jnp.float32
    )
    total_nodes = clusters * lax.axis_size("node") * cluster_rows
    weight_grad = lax.psum(partial_grad, "node") * (1.0 / math.sqrt(total_nodes))
    return (hidden, grad_features, weight_grad)


def solution(mesh):
    return jax.shard_map(
        body,
        mesh=mesh,
        in_specs=(
            P("feat", "node", None),
            P("feat", None),
            P(),
            P("node", "feat", None, None, None),
            P("node", "feat", None),
            P("node", "feat"),
            P("node", "feat", None),
        ),
        out_specs=(P("node", "feat", None), P("feat", "node", None), P("feat", None)),
        check_vma=False,
    )
```

profile of v0, /device:TPU:0, one launch (start us, length us, event | category | flops | bytes accessed | tf_op | source)
XLA Modules:
  0.0 150.2 jit_solution(10850708865901555610)
XLA Ops:
  7.2 0.9 copy-done
  8.1 2.1 %convolution_bitcast_fusion = f32[1024,1,256]{0,2,1:T(8,128)} fusion(bf16[128,256]{1,0:T(8,128)(2,1)} %param.8, bf16[128,1,1024]{2,0,1:T(8,128)(2,1)S(1)} %copy-done), kind=kOutput, calls=%fused_computation.2 | convolution fusion | flops 67108864 | bytes 1376256 | tf_op jit(solution)/shard_map/fqr,fh->rqh/dot_general | solution.py:18
  11.0 0.2 copy-done.1
  11.4 0.6 copy-done.5
  12.1 33.3 %reduce-scatter.2.cloned.1.call-done = f32[128,1,256]{0,2,1:T(8,128)} async-done(((f32[1024,1,256]{0,2,1:T(8,128)}), f32[128,1,256]{0,2,1:T(8,128)}) %reduce-scatter.2.cloned.1.call-update) | async-done | bytes 131088 | tf_op jit(solution)/shard_map/reduce_scatter | solution.py:17
  45.5 0.9 convert_element_type.64
  46.4 14.0 %all-gather = bf16[1024,1,256]{0,2,1:T(8,128)(2,1)S(1)} all-gather(bf16[128,1,256]{0,2,1:T(8,128)(2,1)S(1)} %convert_element_type.64), channel_id=2, replica_groups=mesh['feat'=8,'node'=4] {'feat'}, dimensions={0}, use_global_device_ids=true | all-gather | bytes 589824 | tf_op jit(solution)/shard_map/all_gather | solution.py:25
  60.6 0.6 gather_fusion
  61.3 0.3 fusion.2
  61.5 0.6 copy-done.4
  62.1 0.4 convolution_convert_fusion
  62.5 0.8 broadcast.100
  63.4 2.5 %scatter_fusion = bf16[8,128,256]{2,1,0:T(8,128)(2,1)} fusion(bf16[8,128,256]{2,1,0:T(8,128)(2,1)} %broadcast.100, s32[8]{0:T(128)S(1)} %fusion.32, bf16[8,128,256]{2,1,0:T(8,128)(2,1)S(1)} %convolution_convert_fusion), kind=kCustom, calls=%fused_computation.1 | custom fusion | bytes 1572896 | tf_op jit(solution)/shard_map/scatter | solution.py:49
  65.8 3.5 %all-to-all-start = ((bf16[8,1,128,256]{3,2,1,0:T(8,128)(2,1)}), bf16[8,1,128,256]{3,2,1,0:T(8,128)(2,1)S(1)}, u32[]{:S(2)}, u32[]{:S(2)}) async-start(bf16[8,1,128,256]{3,2,1,0:T(8,128)(2,1)} %bitcast.21), calls=%async_computation.1 | async-start | bytes 1048576 | tf_op jit(solution)/shard_map/all_to_all | solution.py:51
  69.4 0.7 fusion.31
  70.0 14.6 %all-to-all-done = bf16[8,1,128,256]{3,2,1,0:T(8,128)(2,1)S(1)} async-done(((bf16[8,1,128,256]{3,2,1,0:T(8,128)(2,1)}), bf16[8,1,128,256]{3,2,1,0:T(8,128)(2,1)S(1)}, u32[]{:S(2)}, u32[]{:S(2)}) %all-to-all-start) | async-done | bytes 524320 | tf_op jit(solution)/shard_map/all_to_all | solution.py:51
  84.7 14.9 %all-gather.1 = bf16[1024,256]{1,0:T(8,128)(2,1)S(1)} all-gather(bf16[128,256]{1,0:T(8,128)(2,1)S(1)} %reduce_sum.24), channel_id=3, replica_groups=mesh['feat'=8,'node'=4] {'feat'}, dimensions={0}, use_global_device_ids=true | all-gather | bytes 589824 | tf_op jit(solution)/shard_map/all_gather | solution.py:53
  99.6 1.0 convolution_bitcast_fusion.1
  100.6 0.8 copy-done.2
  101.5 0.3 fusion
  101.8 0.9 copy.19
  102.6 39.1 %all-reduce.4.cloned.1.call-done = f32[128,256]{0,1:T(8,128)} async-done(((f32[128,256]{0,1:T(8,128)}), f32[128,256]{0,1:T(8,128)}) %all-reduce.4.cloned.1.call-update) | async-done | bytes 131088 | tf_op jit(solution)/shard_map/psum | solution.py:61
  141.7 0.9 broadcast_multiply_fusion
  142.6 0.8 copy.20
  (20 shorter events, 0.7 us)
Async XLA Ops:
  7.2 1.0 copy-start
  7.2 38.3 %reduce-scatter.2.cloned.1.call-start = ((), (), s32[]{:S(2)}) async-start(), calls=%async_computation.2 | async-start | bytes 1179648 | tf_op jit(solution)/shard_map/reduce_scatter | solution.py:17
  10.3 1.0 copy-start.1
  11.4 0.7 copy-start.5
  60.6 0.7 copy-start.3
  61.3 0.8 copy-start.4
  65.8 18.8 %all-to-all-start = ((bf16[8,1,128,256]{3,2,1,0:T(8,128)(2,1)}), bf16[8,1,128,256]{3,2,1,0:T(8,128)(2,1)S(1)}, u32[]{:S(2)}, u32[]{:S(2)}) async-start(bf16[8,1,128,256]{3,2,1,0:T(8,128)(2,1)} %bitcast.21), calls=%async_computation.1 | async-start | bytes 1048576 | tf_op jit(solution)/shard_map/all_to_all | solution.py:51
  69.3 72.4 %all-reduce.4.cloned.1.call-start = ((), (), s32[]{:S(2)}) async-start(), calls=%async_computation.3 | async-start | bytes 262144 | tf_op jit(solution)/shard_map/psum | solution.py:61
  100.6 0.8 copy-start.2
Sparse Core Ops, SparseCore 0:
  10.4 35.0 reduce-scatter.1
  100.8 40.8 all-reduce.3
where the time goes:
time: 151 us; the launch traced here: 150 us
  waiting for transfers between devices  87 us (58%)
  blocking collectives  28.9 us (19%)
  between operations  14.8 us (10%)
  local copies, waits for them, and re-layouts  8.93 us (6%)
  matrix products  4.12 us (3%)
  starting transfers between devices  3.57 us (2%)
  other arithmetic  2.8 us (2%)
    psum x1, waiting for transfers between devices, body(): lax.psum(partial_grad, 'node') * (1.0 / math.sqrt(total_nodes))  39.1 us
    reduce_scatter x1, waiting for transfers between devices, body(): lax.psum_scatter(jnp.einsum('fqr,fh->rqh', node_features, weight, preferr...  33.3 us
    all_gather x1, blocking collectives, body(): all_grad = lax.all_gather(own_grad, 'feat', axis=1, tiled=True)  14.9 us
    all_to_all x1, waiting for transfers between devices, body(): lax.all_to_all(outgoing, 'feat', split_axis=0, concat_axis=0, tiled=True)  14.6 us
    all_gather x1, blocking collectives, body(): all_proj = lax.all_gather(own_rounded, 'feat', axis=1, tiled=True)  14 us
    unnamed x14, local copies, waits for them, and re-layouts  4.86 us
    all_to_all x1, starting transfers between devices, body(): lax.all_to_all(outgoing, 'feat', split_axis=0, concat_axis=0, tiled=True)  3.49 us
  transfers between devices with their start and end apart: 3, of which 3 were waited for; matrix products, arithmetic and copies ran while one was open for 1% of the time, Pallas kernels for 0%

commit v1 on v0

--- a/solution.py
+++ b/solution.py
@@ -58,7 +58,11 @@
         "fqr,qrh->fh", node_features, all_grad, preferred_element_type=jnp.float32
     )
     total_nodes = clusters * lax.axis_size("node") * cluster_rows
-    weight_grad = lax.psum(partial_grad, "node") * (1.0 / math.sqrt(total_nodes))
+
+    def body_handle(row_data, axis_name):
+        return lax.all_gather(row_data, axis_name=axis_name).sum(axis=0)
+
+    weight_grad = body_handle(partial_grad, "node") * (1.0 / math.sqrt(total_nodes))
     return (hidden, grad_features, weight_grad)
 
 

time: 151 us -> 125 us (0.83)
  waiting for transfers between devices: 87 us -> 48 us
  blocking collectives: 28.9 us -> 43.7 us
    psum x1 -> x0, waiting for transfers between devices: 39.1 us -> none  [body(): lax.psum(partial_grad, 'node') * (1.0 / math.sqrt(total_nodes))]
    all_gather x0 -> x1, blocking collectives: none -> 14.6 us  [body_handle(): return lax.all_gather(row_data, axis_name=axis_name).sum(axis=0)]
  transfers between devices with their start and end apart: 3 -> 2, of which waited for: 3 -> 2; matrix products, arithmetic and copies ran while one was open for 1% -> 1% of each run, Pallas kernels for 0% -> 0%
where the time goes in v1:
time: 125 us; the launch traced here: 124 us
  waiting for transfers between devices  48 us (38%)
  blocking collectives  43.7 us (35%)
  between operations  14.8 us (12%)
  local copies, waits for them, and re-layouts  8.32 us (7%)
  starting transfers between devices  3.53 us (3%)
  matrix products  3.48 us (3%)
  other arithmetic  2.21 us (2%)
    reduce_scatter x1, waiting for transfers between devices, body(): lax.psum_scatter(jnp.einsum('fqr,fh->rqh', node_features, weight, preferr...  33.3 us
    all_gather x1, blocking collectives, body(): all_grad = lax.all_gather(own_grad, 'feat', axis=1, tiled=True)  15.1 us
    all_gather x1, blocking collectives, body_handle(): return lax.all_gather(row_data, axis_name=axis_name).sum(axis=0)  14.6 us
    all_to_all x1, waiting for transfers between devices, body(): lax.all_to_all(outgoing, 'feat', split_axis=0, concat_axis=0, tiled=True)  14.6 us
    all_gather x1, blocking collectives, body(): all_proj = lax.all_gather(own_rounded, 'feat', axis=1, tiled=True)  14 us
    unnamed x14, local copies, waits for them, and re-layouts  4.05 us
    all_to_all x1, starting transfers between devices, body(): lax.all_to_all(outgoing, 'feat', split_axis=0, concat_axis=0, tiled=True)  3.49 us
  transfers between devices with their start and end apart: 2, of which 2 were waited for; matrix products, arithmetic and copies ran while one was open for 1% of the time, Pallas kernels for 0%

profile of v1, /device:TPU:0, one launch (start us, length us, event | category | flops | bytes accessed | tf_op | source)
XLA Modules:
  0.0 124.0 jit_solution(9725458275251633817)
XLA Ops:
  7.2 0.9 copy-done
  8.1 2.1 %convolution_bitcast_fusion = f32[1024,1,256]{0,2,1:T(8,128)} fusion(bf16[128,256]{1,0:T(8,128)(2,1)} %param.8, bf16[128,1,1024]{2,0,1:T(8,128)(2,1)S(1)} %copy-done), kind=kOutput, calls=%fused_computation.2 | convolution fusion | flops 67108864 | bytes 1376256 | tf_op jit(solution)/shard_map/fqr,fh->rqh/dot_general | solution.py:18
  11.0 0.2 copy-done.1
  11.4 0.6 copy-done.5
  12.1 33.3 %reduce-scatter.2.cloned.1.call-done = f32[128,1,256]{0,2,1:T(8,128)} async-done(((f32[1024,1,256]{0,2,1:T(8,128)}), f32[128,1,256]{0,2,1:T(8,128)}) %reduce-scatter.2.cloned.1.call-update) | async-done | bytes 131088 | tf_op jit(solution)/shard_map/reduce_scatter | solution.py:17
  45.5 0.9 convert_element_type.64
  46.4 14.0 %all-gather = bf16[1024,1,256]{0,2,1:T(8,128)(2,1)S(1)} all-gather(bf16[128,1,256]{0,2,1:T(8,128)(2,1)S(1)} %convert_element_type.64), channel_id=2, replica_groups=mesh['feat'=8,'node'=4] {'feat'}, dimensions={0}, use_global_device_ids=true | all-gather | bytes 589824 | tf_op jit(solution)/shard_map/all_gather | solution.py:25
  60.4 0.2 copy.20
  60.6 0.6 gather_fusion
  61.3 0.3 fusion.2
  61.6 0.6 copy-done.4
  62.1 0.4 convolution_convert_fusion
  62.5 0.8 broadcast.100
  63.4 2.5 %scatter_fusion = bf16[8,128,256]{2,1,0:T(8,128)(2,1)} fusion(bf16[8,128,256]{2,1,0:T(8,128)(2,1)} %broadcast.100, s32[8]{0:T(128)S(1)} %fusion.32, bf16[8,128,256]{2,1,0:T(8,128)(2,1)S(1)} %convolution_convert_fusion), kind=kCustom, calls=%fused_computation.1 | custom fusion | bytes 1572896 | tf_op jit(solution)/shard_map/scatter | solution.py:49
  65.8 3.5 %all-to-all-start = ((bf16[8,1,128,256]{3,2,1,0:T(8,128)(2,1)}), bf16[8,1,128,256]{3,2,1,0:T(8,128)(2,1)S(1)}, u32[]{:S(2)}, u32[]{:S(2)}) async-start(bf16[8,1,128,256]{3,2,1,0:T(8,128)(2,1)} %bitcast.21), calls=%async_computation.1 | async-start | bytes 1048576 | tf_op jit(solution)/shard_map/all_to_all | solution.py:51
  69.3 0.7 fusion.31
  70.0 14.6 %all-to-all-done = bf16[8,1,128,256]{3,2,1,0:T(8,128)(2,1)S(1)} async-done(((bf16[8,1,128,256]{3,2,1,0:T(8,128)(2,1)}), bf16[8,1,128,256]{3,2,1,0:T(8,128)(2,1)S(1)}, u32[]{:S(2)}, u32[]{:S(2)}) %all-to-all-start) | async-done | bytes 524320 | tf_op jit(solution)/shard_map/all_to_all | solution.py:51
  84.7 15.1 %all-gather.1 = bf16[1024,256]{1,0:T(8,128)(2,1)S(1)} all-gather(bf16[128,256]{1,0:T(8,128)(2,1)S(1)} %reduce_sum.33), channel_id=3, replica_groups=mesh['feat'=8,'node'=4] {'feat'}, dimensions={0}, use_global_device_ids=true | all-gather | bytes 589824 | tf_op jit(solution)/shard_map/all_gather | solution.py:53
  99.8 0.3 fusion
  100.1 0.3 convolution_bitcast_fusion.1
  100.4 0.9 copy.17
  101.3 14.6 %all-gather.2 = f32[512,256]{0,1:T(8,128)S(1)} all-gather(f32[128,256]{0,1:T(8,128)S(1)} %convolution_bitcast_fusion.1), channel_id=4, replica_groups=mesh['feat'=8,'node'=4] {'node'}, dimensions={0}, use_global_device_ids=true | all-gather | bytes 655360 | tf_op jit(solution)/shard_map/all_gather | solution.py:63
  116.1 0.3 reduce_sum.35
  116.4 0.8 copy.18
  (20 shorter events, 0.7 us)
Async XLA Ops:
  7.2 1.0 copy-start
  7.2 38.3 %reduce-scatter.2.cloned.1.call-start = ((), (), s32[]{:S(2)}) async-start(), calls=%async_computation.2 | async-start | bytes 1179648 | tf_op jit(solution)/shard_map/reduce_scatter | solution.py:17
  10.3 1.0 copy-start.1
  11.4 0.7 copy-start.5
  60.6 0.7 copy-start.3
  61.3 0.8 copy-start.4
  65.8 18.8 %all-to-all-start = ((bf16[8,1,128,256]{3,2,1,0:T(8,128)(2,1)}), bf16[8,1,128,256]{3,2,1,0:T(8,128)(2,1)S(1)}, u32[]{:S(2)}, u32[]{:S(2)}) async-start(bf16[8,1,128,256]{3,2,1,0:T(8,128)(2,1)} %bitcast.21), calls=%async_computation.1 | async-start | bytes 1048576 | tf_op jit(solution)/shard_map/all_to_all | solution.py:51
  84.7 15.1 %copy-start.2 = (bf16[128,256]{1,0:T(8,128)(2,1)S(1)}, bf16[128,256]{1,0:T(8,128)(2,1)}, u32[]{:S(2)}) copy-start(bf16[128,256]{1,0:T(8,128)(2,1)} %param.8) | copy-start | bytes 196612
Sparse Core Ops, SparseCore 0:
  10.4 35.0 reduce-scatter.1
